TPU v7x, 32 devices: a whole 2x2x4 slice. The times are simulated.
32 devices in a mesh: seg: 4 (over z), blk: 8 (over y, x, core).
Axes of the slice: x: 2, y: 2, z: 4, core: 2. Of those that a mesh axis runs over, the one named last changes fastest.
Arguments:
- train_acts: bfloat16 [4, 1024, 512], P('seg', 'blk'), may hold values from -6 to 6
- train_grads: bfloat16 [4, 1024, 4096], P('seg', 'blk'), may hold values from -0.0059814453 to 0.0059814453
- counts: int32 [8], replicated, may hold values from 1 to 2, as said below
- basis_in: bfloat16 [4, 1, 512, 512], P('seg'), may hold values from -1 to 1, as said below
- basis_out: bfloat16 [4, 8, 512, 512], P('seg', 'blk'), may hold values from -1 to 1, as said below
- eigenvalues: bfloat16 [4, 8, 512, 512], P('seg', 'blk'), may hold values from 0.049804688 to 5
- back_weight: bfloat16 [4, 8, 512, 512], P('seg', 'blk'), may hold values from -0.25 to 0.25
- derivative: bfloat16 [4, 4, 32, 4096], P('seg', None, None, 'blk'), may hold values from 0 to 1
- query_acts: bfloat16 [4, 4, 32, 512], P('seg'), may hold values from -6 to 6
- query_top: bfloat16 [4, 32, 4096], P(None, None, 'blk'), may hold values from -0.0059814453 to 0.0059814453
Outputs:
- scores: float32 [4, 16], P(None, 'blk')
Inputs may be any that keep to these rules, and one draw needn't show every extreme that they name: In each pair of indices 2k and 2k+1 of blk one count is 2 and the other 1, so all counts add up to 12; slots below a device's count are valid. `basis_in`: each 512 x 512 matrix is orthogonal up to rounding. `basis_out`: each 512 x 512 matrix is orthogonal up to rounding.
All inputs are finite; a program needn't handle non-finite values.
Results may differ from a plain program's by a relative error of at most 0.015.
Values may be sent and summed in bfloat16 or wider, within the bound.
A program may use at most 64 MiB of HBM per device.

v0:
```python
import functools

import jax
import jax.numpy as jnp
from jax import lax
from jax.experimental import pallas as pl
from jax.experimental.pallas import tpu as pltpu
from jax.sharding import PartitionSpec as P

SLOTS = 2
damping = 0.05
F32 = jnp.float32
B16 = jnp.bfloat16
MESH = pl.DeviceIdType.MESH


def kernel(
    segs,
    blks,
    queries,
    counts,
    acts_h,
    grads_h,
    bin_h,
    bout_h,
    eig_h,
    back_h,
    deriv_h,
    qacts_h,
    qtop_h,
    out,
    acts,
    own_g,
    other_g,
    other_a,
    b_in,
    b_out,
    eig,
    back,
    deriv,
    qacts,
    errs,
    moved,
    inv,
    rot_q,
    core_all,
    grads0,
    grads1,
    racts0,
    racts1,
    turned0,
    part,
    packed,
    gathered,
    load_sem,
    sel_send,
    sel_recv,
    g0_send,
    g0_recv,
    g1_send,
    g1_recv,
    a0_send,
    a0_recv,
    a1_send,
    a1_recv,
    f0_send,
    f1_send,
    e_send,
    e_recv,
    p_send,
    p_recv,
    ready,
):
    seg = lax.axis_index("seg")
    blk = lax.axis_index("blk")
    chips = blks // 2
    chip = blk // 2
    lane = blk % 2
    mate_lane = 1 - lane
    mate = chip * 2 + mate_lane
    rows = acts_h.shape[0]
    tb = rows // SLOTS
    half = tb // 2
    width = bin_h.shape[0]
    qt = qtop_h.shape[0] // queries

    def remote(src, dst, ssem, rsem, seg_to, blk_to):
        return pltpu.make_async_remote_copy(
            src_ref=src,
            dst_ref=dst,
            send_sem=ssem,
            recv_sem=rsem,
            device_id=(seg_to, blk_to),
            device_id_type=MESH,
        )

    def cols(index):
        return pl.ds(pl.multiple_of(index * width, width), width)

    barrier = pltpu.get_barrier_semaphore()
    for off in range(1, blks):
        pl.semaphore_signal(
            barrier, inc=1, device_id=(seg, lax.rem(blk + off, blks)), device_id_type=MESH
        )
    for off in range(1, segs):
        pl.semaphore_signal(
            barrier, inc=1, device_id=(lax.rem(seg + off, segs), blk), device_id_type=MESH
        )

    keep = pl.ds(pl.multiple_of(tb + lane * half, half), half)
    give = pl.ds(pl.multiple_of(tb + mate_lane * half, half), half)
    mine0 = pl.ds(pl.multiple_of(lane * tb, tb), tb)
    mine1 = pl.ds(pl.multiple_of(lane * half, half), half)

    loads = [
        pltpu.make_async_copy(src, dst, load_sem.at[n])
        for n, (src, dst) in enumerate(
            (
                (back_h, back),
                (deriv_h, deriv),
                (acts_h, acts),
                (bin_h, b_in),
                (grads_h.at[keep, :], own_g),
                (qacts_h, qacts),
                (eig_h, eig),
                (bout_h, b_out),
            )
        )
    ]
    l_back, l_deriv, l_acts, l_bin, l_own, l_qacts, l_eig, l_bout = loads
    l_top = pltpu.make_async_copy(qtop_h, errs, load_sem.at[len(loads)])

    @pl.when(seg == segs - 1)
    def _():
        l_top.start()

    for load in loads:
        load.start()
    own0 = pltpu.make_async_copy(
        grads_h.at[pl.ds(0, tb), cols(blk)], grads0.at[0, mine0], g0_recv.at[0, lane]
    )
    own0.start()

    def e_copy(q):
        r = pl.ds(q * qt, qt)
        return remote(
            moved.at[r],
            errs.at[r],
            e_send.at[q],
            e_recv.at[q],
            lax.rem(seg + segs - 1, segs),
            blk,
        )

    def advance(q):
        r = pl.ds(q * qt, qt)
        e = errs[r]
        mixed = jnp.dot(e, back[...], preferred_element_type=F32)
        moved[r] = (e.astype(F32) + mixed * deriv[r].astype(F32)).astype(B16)

    l_back.wait()
    l_deriv.wait()

    @pl.when(seg == segs - 1)
    def _():
        l_top.wait()
        for q in range(queries):
            advance(q)

    pl.semaphore_wait(barrier, blks - 1 + segs - 1)

    @pl.when(seg == segs - 1)
    def _():
        for q in range(queries):
            e_copy(q).start()

    sends = []

    def send(copy):
        copy.start()
        sends.append(copy)
        return copy

    sel_a = send(remote(acts_h.at[give, :], other_a, sel_send.at[0], sel_recv.at[0], seg, mate))
    sel_g = send(remote(grads_h.at[give, :], other_g, sel_send.at[1], sel_recv.at[1], seg, mate))

    def to_chip(off):
        return lax.rem(chip + off, chips)

    def targets():
        for off in range(1, chips):
            for side in range(2):
                yield off, side, to_chip(off) * 2 + side
        yield 0, 0, mate

    def act_targets():
        for off in range(1, chips):
            yield off, to_chip(off) * 2 + lane
        yield 0, mate

    for off, side, dest in targets():
        send(
            remote(
                grads_h.at[pl.ds(0, tb), cols(dest)],
                grads0.at[off, mine0],
                g0_send.at[off, side],
                g0_recv.at[off, lane],
                seg,
                dest,
            )
        )
    l_acts.wait()
    l_bin.wait()
    racts0[0, mine0] = jnp.dot(acts[0:tb], b_in[...], preferred_element_type=F32).astype(B16)

    for off, dest in act_targets():
        send(
            remote(
                racts0.at[0, mine0],
                racts0.at[off, mine0],
                a0_send.at[off],
                a0_recv.at[off, lane],
                seg,
                dest,
            )
        )
    for off in range(1, segs):
        pl.semaphore_signal(
            ready, inc=1, device_id=(lax.rem(seg + off, segs), blk), device_id_type=MESH
        )

    full = counts[blk] == SLOTS
    sel_a.wait_recv()
    picked = jnp.where(full, acts[keep, :].astype(F32), other_a[...].astype(F32)).astype(B16)
    racts1[0, mine1] = jnp.dot(picked, b_in[...], preferred_element_type=F32).astype(B16)
    for off, dest in act_targets():
        send(
            remote(
                racts1.at[0, mine1],
                racts1.at[off, mine1],
                a1_send.at[off],
                a1_recv.at[off, lane],
                seg,
                dest,
            )
        )

    l_own.wait()
    sel_g.wait_recv()
    own_g[...] = jnp.where(full, own_g[...].astype(F32), other_g[...].astype(F32)).astype(B16)
    for off, side, dest in targets():
        send(
            remote(
                own_g.at[:, cols(dest)],
                grads1.at[off, mine1],
                g1_send.at[off, side],
                g1_recv.at[off, lane],
                seg,
                dest,
            )
        )
    own1 = pltpu.make_async_copy(own_g.at[:, cols(blk)], grads1.at[0, mine1], g1_recv.at[0, lane])
    own1.start()

    l_qacts.wait()
    rot_q[...] = jnp.dot(qacts[...], b_in[...], preferred_element_type=F32).astype(B16)
    l_eig.wait()
    inv[...] = 1.0 / (eig[...].astype(F32) + damping)
    l_bout.wait()

    @pl.when(jnp.logical_and(seg > 0, seg < segs - 1))
    def _():
        for q in range(queries):
            e_copy(q).wait_recv()
            advance(q)
            e_copy(q).start()

    def arrived(buf, sem, i, side, size):
        ref = buf.at[i, pl.ds(pl.multiple_of(side * size, size), size)]
        remote(ref, ref, sel_send.at[0], sem.at[i, side], seg, mate).wait_recv()

    def forward(buf, sem, fsem, rows_of, size):
        for off in range(1, chips):
            arrived(buf, sem, off, lane, size)
            ref = buf.at[off, rows_of]
            send(remote(ref, ref, fsem.at[off], sem.at[off, lane], seg, mate))

    forward(racts0, a0_recv, f0_send, mine0, tb)
    for i in range(chips):
        for side in range(2):
            arrived(grads0, g0_recv, i, side, tb)
        turned0[i] = jnp.dot(grads0[i], b_out[...], preferred_element_type=F32).astype(B16)
    forward(racts1, a1_recv, f1_send, mine1, half)
    for i in range(chips):
        arrived(racts0, a0_recv, i, mate_lane, tb)

    def core_of(q):
        return core_all[:, q * width : (q + 1) * width]

    def folded(x):
        x = sum(x[:, n * 128 : (n + 1) * 128] for n in range(width // 128))
        return jnp.sum(x, axis=0, keepdims=True)

    for q in range(queries):

        @pl.when(seg == 0)
        def _():
            e_copy(q).wait_recv()

        r = pl.ds(q * qt, qt)
        rot_e = jnp.dot(errs[r], b_out[...], preferred_element_type=F32).astype(B16)
        raw = lax.dot_general(
            rot_e, rot_q[r], (((0,), (0,)), ((), ())), preferred_element_type=F32
        )
        core_all[:, q * width : (q + 1) * width] = (raw * inv[...]).astype(B16)
        for i in range(chips):
            h = jnp.dot(turned0[i], core_of(q), preferred_element_type=F32)
            prod = h * racts0[i].astype(F32)
            for side in range(2):
                part[i, side, q : q + 1, :] = folded(prod[side * tb : (side + 1) * tb])

    for i in range(chips):
        for side in range(2):
            arrived(grads1, g1_recv, i, side, half)
        arrived(racts1, a1_recv, i, mate_lane, half)
    late = jnp.dot(
        grads1[...].reshape(chips * tb, width), b_out[...], preferred_element_type=F32
    ).astype(B16)
    for q in range(queries):
        h = jnp.dot(late, core_of(q), preferred_element_type=F32)
        prod = h * racts1[...].reshape(chips * tb, width).astype(F32)
        for i in range(chips):
            shared = folded(prod[i * tb : (i + 1) * tb])
            for side in range(2):
                part[i, side, queries + q : queries + q + 1, :] = shared

    values = 2 * queries
    tile = (chips, 2, values, 128)
    diag = lax.broadcasted_iota(jnp.int32, tile, 2) == lax.broadcasted_iota(jnp.int32, tile, 3)
    sums = jnp.sum(part[...], axis=3, keepdims=True)
    packed[...] = jnp.sum(jnp.where(diag, sums, 0.0), axis=2, keepdims=True)

    pl.semaphore_wait(ready, segs - 1)
    for seg_off in range(segs - 1, -1, -1):
        seg_to = lax.rem(seg + seg_off, segs)
        for off in range(chips):
            chip_to = lax.rem(chip + chips - off, chips)
            for turn in range(2):
                if seg_off == 0 and off == 0 and turn == 0:
                    continue
                side = lane if turn == 0 else mate_lane
                send(
                    remote(
                        packed.at[off, side],
                        gathered.at[seg, blk],
                        p_send.at[seg_off, off, turn],
                        p_recv.at[seg, blk],
                        seg_to,
                        chip_to * 2 + side,
                    )
                )
    gathered[seg, blk] = packed[0, lane]
    for seg_off in range(segs):
        for off in range(blks):
            if seg_off == 0 and off == 0:
                continue
            a, b = lax.rem(seg + seg_off, segs), lax.rem(blk + off, blks)
            ref = gathered.at[a, b]
            remote(ref, ref, sel_send.at[0], p_recv.at[a, b], seg, mate).wait_recv()
    total = jnp.sum(gathered[...].reshape(segs * blks, 128), axis=0, keepdims=True)
    tile = (values, 128)
    diag = lax.broadcasted_iota(jnp.int32, tile, 0) == lax.broadcasted_iota(jnp.int32, tile, 1)
    total = jnp.sum(jnp.where(diag, jnp.broadcast_to(total, tile), 0.0), axis=1, keepdims=True)
    out[:, 0:1] = total[0:queries]
    out[:, 1:2] = total[queries:values] * jnp.where(full, 1.0, 0.0)

    for copy in sends:
        copy.wait_send()

    @pl.when(seg > 0)
    def _():
        for q in range(queries):
            e_copy(q).wait_send()


def body(
    train_acts,
    train_grads,
    counts,
    basis_in,
    basis_out,
    eigenvalues,
    back_weight,
    derivative,
    query_acts,
    query_top,
):
    segs = lax.axis_size("seg")
    blks = lax.axis_size("blk")
    chips = blks // 2
    queries, qt, width = query_top.shape
    rows = train_acts.shape[1]
    tb = rows // SLOTS
    half = tb // 2
    wide = train_grads.shape[2]
    any_spec = pl.BlockSpec(memory_space=pltpu.HBM)
    vm = pltpu.VMEM
    dma = pltpu.SemaphoreType.DMA
    return pl.pallas_call(
        functools.partial(kernel, segs, blks, queries),
        out_shape=jax.ShapeDtypeStruct((queries, SLOTS), F32),
        in_specs=[pl.BlockSpec(memory_space=pltpu.SMEM)] + [any_spec] * 9,
        out_specs=pl.BlockSpec(memory_space=pltpu.VMEM),
        scratch_shapes=[
            vm((rows, width), B16),
            vm((half, wide), B16),
            vm((half, wide), B16),
            vm((half, width), B16),
            vm((width, width), B16),
            vm((width, width), B16),
            vm((width, width), B16),
            vm((width, width), B16),
            vm((queries * qt, width), B16),
            vm((queries * qt, width), B16),
            vm((queries * qt, width), B16),
            vm((queries * qt, width), B16),
            vm((width, width), F32),
            vm((queries * qt, width), B16),
            vm((width, queries * width), B16),
            vm((chips, 2 * tb, width), B16),
            vm((chips, 2 * half, width), B16),
            vm((chips, 2 * tb, width), B16),
            vm((chips, 2 * half, width), B16),
            vm((chips, 2 * tb, width), B16),
            vm((chips, 2, 2 * queries, 128), F32),
            vm((chips, 2, 1, 128), F32),
            vm((segs, blks, 1, 128), F32),
            dma((9,)),
            dma((2,)),
            dma((2,)),
            dma((chips, 2)),
            dma((chips, 2)),
            dma((chips, 2)),
            dma((chips, 2)),
            dma((chips,)),
            dma((chips, 2)),
            dma((chips,)),
            dma((chips, 2)),
            dma((chips,)),
            dma((chips,)),
            dma((queries,)),
            dma((queries,)),
            dma((segs, chips, 2)),
            dma((segs, blks)),
            pltpu.SemaphoreType.REGULAR,
        ],
        compiler_params=pltpu.CompilerParams(
            collective_id=0, has_side_effects=True, vmem_limit_bytes=67_043_328
        ),
    )(
        counts,
        train_acts[0],
        train_grads[0],
        basis_in[0, 0],
        basis_out[0, 0],
        eigenvalues[0, 0],
        back_weight[0, 0],
        derivative[0].reshape(queries * qt, width),
        query_acts[0].reshape(queries * qt, width),
        query_top.reshape(queries * qt, width),
    )


def solution(mesh):
    in_specs = (
        P("seg", "blk", None),
        P("seg", "blk", None),
        P(),
        P("seg", None, None, None),
        P("seg", "blk", None, None),
        P("seg", "blk", None, None),
        P("seg", "blk", None, None),
        P("seg", None, None, "blk"),
        P("seg", None, None, None),
        P(None, None, "blk"),
    )
    out_specs = P(None, "blk")
    return jax.shard_map(body, mesh=mesh, in_specs=in_specs, out_specs=out_specs, check_vma=False)
```

profile of v0, /device:TPU:0, one launch (start us, length us, event | category | flops | bytes accessed | tf_op | source)
XLA Modules:
  0.0 32.1 jit_solution(9520679499389063699)
XLA Ops:
  0.0 30.7 %shard_map.100 = f32[4,2]{1,0:T(4,128)} custom-call(s32[8]{0:T(128)} %counts.1, bf16[128,512]{1,0:T(8,128)(2,1)} %bitcast.14, bf16[128,4096]{1,0:T(8,128)(2,1)} %bitcast.9, bf16[512,512]{1,0:T(8,128)(2,1)} %bitcast.10, bf16[512,512]{1,0:T(8,128)(2,1)} %bitcast.11, bf16[512,512]{1,0:T(8,128)(2,1)} %bitcast.12, bf16[512,512]{1,0:T(8,128)(2,1)} %bitcast.13, ...), custom_call_target="tpu_custom_call" | custom-call | tf_op jit(solution)/shard_map/pallas_call | solution.py:409
  30.8 1.3 %copy.11 = f32[4,2]{0,1:T(2,128)} copy(f32[4,2]{1,0:T(4,128)} %shard_map.100) | data formatting | bytes 64 | tf_op jit(solution)/shard_map/pallas_call | solution.py:409
where the time goes:
time: 32.2 us; the launch traced here: 32.1 us
  Pallas kernels  30.7 us (95%)
  local copies, waits for them, and re-layouts  1.32 us (4%)
    pallas_call x1, Pallas kernels, body(): pl.pallas_call(functools.partial(kernel, segs, blks, queries), out_shape=...  30.7 us
    pallas_call x1, local copies, waits for them, and re-layouts, body(): pl.pallas_call(functools.partial(kernel, segs, blks, queries), out_shape=...  1.32 us

commit v1 on v0

v1 whole, which is shorter than its diff:
```python
import functools

import jax
import jax.numpy as jnp
from jax import lax
from jax.experimental import pallas as pl
from jax.experimental.pallas import tpu as pltpu
from jax.sharding import PartitionSpec as P

SLOTS = 2
HALVES = 2
damping = 0.05
F32 = jnp.float32
B16 = jnp.bfloat16
MESH = pl.DeviceIdType.MESH


def kernel(
    segs,
    blks,
    queries,
    counts_h,
    acts_h,
    grads_h,
    bin_h,
    bout_h,
    eig_h,
    back_h,
    deriv_h,
    qacts_h,
    qtop_h,
    out,
    counts,
    acts,
    own_g,
    other_g,
    other_a,
    b_in,
    b_out,
    eig,
    back,
    deriv,
    qacts,
    errs,
    moved,
    rot_q,
    core_all,
    grads0,
    grads1,
    racts,
    part,
    packed,
    gathered,
    load_sem,
    sel_recv,
    g0_send,
    g0_recv,
    g1_send,
    g1_recv,
    a_send,
    a_recv,
    am_recv,
    e_send,
    e_recv,
    p_send,
    p_recv,
    ready,
):
    seg = lax.axis_index("seg")
    blk = lax.axis_index("blk")
    chips = blks // 2
    steps = chips.bit_length() - 1
    chip = blk // 2
    lane = blk % 2
    mate_lane = 1 - lane
    mate = chip * 2 + mate_lane
    rows = acts_h.shape[0]
    tb = rows // SLOTS
    half = tb // 2
    block = tb + half
    width = bin_h.shape[0]
    qrows = qtop_h.shape[0]
    qt = qrows // queries
    piece = qrows // HALVES

    barrier = pltpu.get_barrier_semaphore()
    for off in range(1, blks):
        pl.semaphore_signal(
            barrier, inc=1, device_id=(seg, lax.rem(blk + off, blks)), device_id_type=MESH
        )
    for off in range(1, segs):
        pl.semaphore_signal(
            barrier, inc=1, device_id=(lax.rem(seg + off, segs), blk), device_id_type=MESH
        )

    def flip(c, bit):
        return c + bit * (1 - 2 * lax.rem(c // bit, 2))

    def chip_at(off):
        c = chip
        for j in range(steps):
            if off >> j & 1:
                c = flip(c, 1 << j)
        return c

    low = [1 << j for j in range(steps)]
    high = low[::-1]
    bits = [a + lane * (b - a) for a, b in zip(low, high)]
    partners = [flip(chip, a) + lane * (flip(chip, b) - flip(chip, a)) for a, b in zip(low, high)]

    def slot_of(code):
        return sum((bits[j] for j in range(steps) if code >> j & 1), 0)

    def remote(src, dst, ssem, rsem, seg_to, blk_to):
        return pltpu.make_async_remote_copy(
            src_ref=src,
            dst_ref=dst,
            send_sem=ssem,
            recv_sem=rsem,
            device_id=(seg_to, blk_to),
            device_id_type=MESH,
        )

    def cols(index):
        return pl.ds(pl.multiple_of(index * width, width), width)

    def span(index, size):
        return pl.ds(pl.multiple_of(index * size, size), size)

    def landed(ref, sem):
        remote(ref, ref, g0_send, sem, seg, mate).wait_recv()

    def loaded(ref, sem):
        pltpu.make_async_copy(ref, ref, sem).wait()

    def racts_at(slot, side):
        return racts.at[span(slot * 2 + side, block)]

    keep = pl.ds(pl.multiple_of(tb + lane * half, half), half)
    give = pl.ds(pl.multiple_of(tb + mate_lane * half, half), half)

    l_top = pltpu.make_async_copy(qtop_h, errs, load_sem.at[0])

    @pl.when(seg == segs - 1)
    def _():
        l_top.start()

    for src, dst, n in (
        (back_h, back, 1),
        (deriv_h, deriv, 1),
        (acts_h, acts, 2),
        (bin_h, b_in, 2),
        (counts_h, counts, 3),
        (grads_h.at[keep, :], own_g, 4),
        (bout_h, b_out, 5),
        (qacts_h, qacts, 5),
        (eig_h, eig, 6),
        (grads_h.at[pl.ds(0, tb), cols(blk)], grads0.at[span(lane, tb)], None),
    ):
        sem = g0_recv.at[0] if n is None else load_sem.at[n]
        pltpu.make_async_copy(src, dst, sem).start()

    def e_copy(n):
        r = pl.ds(n * piece, piece)
        below = lax.rem(seg + segs - 1, segs)
        return remote(moved.at[r], errs.at[r], e_send, e_recv.at[n], below, blk)

    def advance(n):
        r = pl.ds(n * piece, piece)
        e = errs[r]
        mixed = jnp.dot(e, back[...], preferred_element_type=F32)
        moved[r] = (e.astype(F32) + mixed * deriv[r].astype(F32)).astype(B16)

    @pl.when(seg == segs - 1)
    def _():
        loaded(racts.at[pl.ds(0, width + qrows)], load_sem.at[1])
        l_top.wait()
        for n in range(HALVES):
            advance(n)

    pl.semaphore_wait(barrier, blks - 1 + segs - 1)

    @pl.when(seg == segs - 1)
    def _():
        for n in range(HALVES):
            e_copy(n).start()

    remote(acts_h.at[give, :], other_a, g1_send, sel_recv.at[0], seg, mate).start()
    remote(grads_h.at[give, :], other_g, g1_send, sel_recv.at[1], seg, mate).start()

    def send0(off, side):
        dest = chip_at(off) * 2 + side
        remote(
            grads_h.at[pl.ds(0, tb), cols(dest)],
            grads0.at[span(off * 2 + lane, tb)],
            g0_send,
            g0_recv.at[off],
            seg,
            dest,
        ).start()

    def send1(off, side):
        dest = chip_at(off) * 2 + side
        remote(
            own_g.at[:, cols(dest)],
            grads1.at[span(off * 2 + lane, half)],
            g1_send,
            g1_recv,
            seg,
            dest,
        ).start()

    near = list(low)
    far = [off for off in range(1, chips) if off not in near]
    for off in near:
        send0(off, lane)

    loaded(racts.at[pl.ds(0, width + rows)], load_sem.at[2])
    loaded(counts, load_sem.at[3])
    full = counts[blk] == SLOTS
    landed(other_a, sel_recv.at[0])
    acts[tb : tb + half] = jnp.where(
        full, acts[keep, :].astype(F32), other_a[...].astype(F32)
    ).astype(B16)
    mine = span(lane, block)
    racts[mine] = jnp.dot(acts[0:block], b_in[...], preferred_element_type=F32).astype(B16)

    def relay(code):
        slot = slot_of(code)
        src = racts_at(slot, lane)
        for j in range(code.bit_length(), steps):
            to = slot + bits[j]
            dest = partners[j] * 2 + lane
            remote(src, racts_at(to, lane), a_send, a_recv.at[to], seg, dest).start()
        remote(src, src, a_send, am_recv.at[slot], seg, mate).start()

    relay(0)
    for off in near:
        send0(off, mate_lane)
    for off in far:
        send0(off, lane)
        send0(off, mate_lane)
    send0(0, mate_lane)
    for off in range(1, segs):
        pl.semaphore_signal(
            ready, inc=1, device_id=(lax.rem(seg + off, segs), blk), device_id_type=MESH
        )

    loaded(own_g, load_sem.at[4])
    landed(other_g, sel_recv.at[1])
    own_g[...] = jnp.where(full, own_g[...].astype(F32), other_g[...].astype(F32)).astype(B16)

    @pl.when(seg < segs - 1)
    def _():
        loaded(racts.at[pl.ds(0, width + qrows)], load_sem.at[1])

    @pl.when(jnp.logical_and(seg > 0, seg < segs - 1))
    def _():
        for n in range(HALVES):
            landed(errs.at[pl.ds(n * piece, piece)], e_recv.at[n])
            advance(n)
            e_copy(n).start()

    for code in range(1, chips):
        if code.bit_length() == steps and code > 1 << steps - 1:
            continue
        landed(racts_at(slot_of(code), lane), a_recv.at[slot_of(code)])
        relay(code)
    for off in far + near:
        send1(off, lane)
        send1(off, mate_lane)
    send1(0, mate_lane)
    own1 = pltpu.make_async_copy(own_g.at[:, cols(blk)], grads1.at[span(lane, half)], g1_recv)
    own1.start()

    loaded(racts.at[pl.ds(0, width + qrows)], load_sem.at[5])
    rot_q[...] = jnp.dot(qacts[...], b_in[...], preferred_element_type=F32).astype(B16)
    loaded(eig, load_sem.at[6])
    inv = 1.0 / (eig[...].astype(F32) + damping)

    @pl.when(seg == 0)
    def _():
        for n in range(HALVES):
            landed(errs.at[pl.ds(n * piece, piece)], e_recv.at[n])

    rot_e = jnp.dot(errs[...], b_out[...], preferred_element_type=F32).astype(B16)
    for q in range(queries):
        r = slice(q * qt, (q + 1) * qt)
        raw = lax.dot_general(
            rot_e[r], rot_q[r], (((0,), (0,)), ((), ())), preferred_element_type=F32
        )
        core_all[:, q * width : (q + 1) * width] = (raw * inv).astype(B16)

    for code in range((1 << steps - 1) + 1, chips):
        landed(racts_at(slot_of(code), lane), a_recv.at[slot_of(code)])
        relay(code)

    def core_of(q):
        return core_all[:, q * width : (q + 1) * width]

    def folded(x):
        x = sum(x[:, n * 128 : (n + 1) * 128] for n in range(width // 128))
        return jnp.sum(x, axis=0, keepdims=True)

    def rows_of(i, side, start, size):
        return racts[pl.ds((i * 2 + side) * block + start, size), :].astype(F32)

    for pair in range(0, chips, 2):
        for i in (pair, pair + 1):
            landed(grads0.at[pl.ds(i * 2 * tb, 2 * tb)], g0_recv.at[i])
            landed(racts_at(i, mate_lane), am_recv.at[i])
        turned = jnp.dot(
            grads0[pl.ds(pair * 2 * tb, 4 * tb), :], b_out[...], preferred_element_type=F32
        ).astype(B16)
        for q in range(queries):
            h = jnp.dot(turned, core_of(q), preferred_element_type=F32)
            for n in range(4):
                i, side = pair + n // 2, n % 2
                prod = h[n * tb : (n + 1) * tb] * rows_of(i, side, 0, tb)
                part[i, side, q : q + 1, :] = folded(prod)

    landed(grads1, g1_recv)
    turned = jnp.dot(grads1[...], b_out[...], preferred_element_type=F32).astype(B16)
    for q in range(queries):
        h = jnp.dot(turned, core_of(q), preferred_element_type=F32)
        for i in range(chips):
            shared = sum(
                folded(
                    h[(i * 2 + side) * half : (i * 2 + side + 1) * half]
                    * rows_of(i, side, tb, half)
                )
                for side in range(2)
            )
            for side in range(2):
                part[i, side, queries + q : queries + q + 1, :] = shared

    values = SLOTS * queries
    tile = (chips, 2, values, 128)
    row = lax.broadcasted_iota(jnp.int32, tile, 2)
    col = lax.broadcasted_iota(jnp.int32, tile, 3)
    sums = jnp.sum(part[...], axis=3, keepdims=True)
    for s in range(SLOTS):
        placed = jnp.where(row == col + s * queries, sums, 0.0)
        placed = jnp.where(col < queries, placed, 0.0)
        packed[:, :, s : s + 1, :] = jnp.sum(placed, axis=2, keepdims=True)

    pl.semaphore_wait(ready, segs - 1)
    for seg_off in range(segs - 1, -1, -1):
        seg_to = lax.rem(seg + seg_off, segs)
        for off in range(chips - 1, -1, -1):
            chip_to = chip_at(off)
            for side in (lane, mate_lane):
                if seg_off == 0 and off == 0 and side is lane:
                    continue
                remote(
                    packed.at[off, side],
                    gathered.at[seg * blks + blk],
                    p_send,
                    p_recv,
                    seg_to,
                    chip_to * 2 + side,
                ).start()
    gathered[seg * blks + blk] = packed[0, lane]
    others = gathered.at[pl.ds(0, segs * blks - 1)]
    landed(others, p_recv)
    total = jnp.sum(gathered[...], axis=0)[:, 0:queries]
    slot = lax.broadcasted_iota(jnp.int32, total.shape, 0)
    out[...] = total * jnp.where(jnp.logical_or(slot == 0, full), 1.0, 0.0)

    remote(others, others, p_send, p_recv, seg, mate).wait_send()

    def sent(count, sem):
        ref = racts.at[pl.ds(0, count)]
        remote(ref, ref, sem, sel_recv.at[0], seg, mate).wait_send()

    sent((blks - 1) * tb, g0_send)
    sent((blks - 1) * half + half + half * blks, g1_send)
    sent((2 * chips - 1) * block, a_send)

    @pl.when(seg > 0)
    def _():
        sent(qrows, e_send)


def body(
    train_acts,
    train_grads,
    counts,
    basis_in,
    basis_out,
    eigenvalues,
    back_weight,
    derivative,
    query_acts,
    query_top,
):
    segs = lax.axis_size("seg")
    blks = lax.axis_size("blk")
    chips = blks // 2
    queries, qt, width = query_top.shape
    rows = train_acts.shape[1]
    tb = rows // SLOTS
    half = tb // 2
    wide = train_grads.shape[2]
    any_spec = pl.BlockSpec(memory_space=pltpu.HBM)
    vm = pltpu.VMEM
    dma = pltpu.SemaphoreType.DMA
    result = pl.pallas_call(
        functools.partial(kernel, segs, blks, queries),
        out_shape=pltpu.VMEM((SLOTS, queries), F32),
        in_specs=[any_spec] * 10,
        out_specs=pl.BlockSpec(memory_space=pltpu.VMEM),
        scratch_shapes=[
            pltpu.SMEM(counts.shape, counts.dtype),
            vm((rows, width), B16),
            vm((half, wide), B16),
            vm((half, wide), B16),
            vm((half, width), B16),
            vm((width, width), B16),
            vm((width, width), B16),
            vm((width, width), B16),
            vm((width, width), B16),
            vm((queries * qt, width), B16),
            vm((queries * qt, width), B16),
            vm((queries * qt, width), B16),
            vm((queries * qt, width), B16),
            vm((queries * qt, width), B16),
            vm((width, queries * width), B16),
            vm((blks * tb, width), B16),
            vm((blks * half, width), B16),
            vm((blks * (tb + half), width), B16),
            vm((chips, 2, SLOTS * queries, 128), F32),
            vm((chips, 2, SLOTS, 128), F32),
            vm((segs * blks, SLOTS, 128), F32),
            dma((7,)),
            dma((2,)),
            dma(()),
            dma((chips,)),
            dma(()),
            dma(()),
            dma(()),
            dma((chips,)),
            dma((chips,)),
            dma(()),
            dma((HALVES,)),
            dma(()),
            dma(()),
            pltpu.SemaphoreType.REGULAR,
        ],
        compiler_params=pltpu.CompilerParams(
            collective_id=0, has_side_effects=True, vmem_limit_bytes=67_043_328 - 32_768
        ),
    )(
        counts,
        train_acts[0],
        train_grads[0],
        basis_in[0, 0],
        basis_out[0, 0],
        eigenvalues[0, 0],
        back_weight[0, 0],
        derivative[0].reshape(queries * qt, width),
        query_acts[0].reshape(queries * qt, width),
        query_top.reshape(queries * qt, width),
    )
    return result.T


def solution(mesh):
    in_specs = (
        P("seg", "blk", None),
        P("seg", "blk", None),
        P(),
        P("seg", None, None, None),
        P("seg", "blk", None, None),
        P("seg", "blk", None, None),
        P("seg", "blk", None, None),
        P("seg", None, None, "blk"),
        P("seg", None, None, None),
        P(None, None, "blk"),
    )
    out_specs = P(None, "blk")
    return jax.shard_map(body, mesh=mesh, in_specs=in_specs, out_specs=out_specs, check_vma=False)
```

time: 32.2 us -> 27.2 us (0.84)
  Pallas kernels: 30.7 us -> 26.5 us
  local copies, waits for them, and re-layouts: 1.32 us -> 0.56 us
    pallas_call x1, Pallas kernels: 30.7 us -> 26.5 us  [body(): pl.pallas_call(functools.partial(kernel, segs, blks, queries), out_shape=...]
    pallas_call x1 -> x0, local copies, waits for them, and re-layouts: 1.32 us -> none  [body(): pl.pallas_call(functools.partial(kernel, segs, blks, queries), out_shape=...]
    unnamed x0 -> x1, local copies, waits for them, and re-layouts: none -> 0.56 us
where the time goes in v1:
time: 27.2 us; the launch traced here: 27.1 us
  Pallas kernels  26.5 us (97%)
  local copies, waits for them, and re-layouts  0.56 us (2%)
    pallas_call x1, Pallas kernels, body(): pl.pallas_call(functools.partial(kernel, segs, blks, queries), out_shape=...  26.5 us
    unnamed x1, local copies, waits for them, and re-layouts  0.56 us

profile of v1, /device:TPU:0, one launch (start us, length us, event | category | flops | bytes accessed | tf_op | source)
XLA Modules:
  0.0 27.1 jit_solution(3515866129070671657)
XLA Ops:
  0.0 26.5 %shard_map.100 = f32[2,4]{1,0:T(2,128)S(1)} custom-call(s32[8]{0:T(128)} %counts_h.1, bf16[128,512]{1,0:T(8,128)(2,1)} %bitcast.16, bf16[128,4096]{1,0:T(8,128)(2,1)} %bitcast.11, bf16[512,512]{1,0:T(8,128)(2,1)} %bitcast.12, bf16[512,512]{1,0:T(8,128)(2,1)} %bitcast.13, bf16[512,512]{1,0:T(8,128)(2,1)} %bitcast.14, bf16[512,512]{1,0:T(8,128)(2,1)} %bitcast.15, ...), custom_call_target="tpu_custom_call" | custom-call | tf_op jit(solution)/shard_map/pallas_call | solution.py:408
  26.5 0.6 %copy.12 = f32[4,2]{0,1:T(2,128)} copy(f32[4,2]{0,1:T(2,128)S(1)} %bitcast.10) | data formatting | bytes 64

commit v2 on v1

v2 whole, which is shorter than its diff:
```python
import functools

import jax
import jax.numpy as jnp
from jax import lax
from jax.experimental import pallas as pl
from jax.experimental.pallas import tpu as pltpu
from jax.sharding import PartitionSpec as P

SLOTS = 2
damping = 0.05
F32 = jnp.float32
B16 = jnp.bfloat16
MESH = pl.DeviceIdType.MESH


def kernel(
    segs,
    blks,
    queries,
    counts_h,
    acts_h,
    grads_h,
    bin_h,
    bout_h,
    eig_h,
    back_h,
    deriv_h,
    qacts_h,
    qtop_h,
    out,
    counts,
    acts,
    own_g,
    other_g,
    other_a,
    b_in,
    b_out,
    eig,
    back,
    deriv,
    qacts,
    errs,
    moved,
    rot_q,
    core_all,
    grads0,
    grads1,
    racts0,
    racts1,
    part,
    packed,
    gathered,
    load_sem,
    sel_recv,
    g0_send,
    g1_send,
    a_send,
    early_recv,
    late_recv,
    a0_recv,
    a1_recv,
    e_send,
    e_recv,
    p_send,
    p_recv,
    ready,
):
    seg = lax.axis_index("seg")
    blk = lax.axis_index("blk")
    chips = blks // 2
    steps = chips.bit_length() - 1
    chip = blk // 2
    lane = blk % 2
    mate_lane = 1 - lane
    mate = chip * 2 + mate_lane
    rows = acts_h.shape[0]
    tb = rows // SLOTS
    half = tb // 2
    width = bin_h.shape[0]
    qrows = qtop_h.shape[0]
    qt = qrows // queries

    barrier = pltpu.get_barrier_semaphore()
    for off in range(1, blks):
        pl.semaphore_signal(
            barrier, inc=1, device_id=(seg, lax.rem(blk + off, blks)), device_id_type=MESH
        )
    above, below = lax.rem(seg + 1, segs), lax.rem(seg + segs - 1, segs)

    @pl.when(seg < segs - 1)
    def _():
        pl.semaphore_signal(barrier, inc=1, device_id=(above, blk), device_id_type=MESH)

    @pl.when(seg > 0)
    def _():
        pl.semaphore_signal(barrier, inc=1, device_id=(below, blk), device_id_type=MESH)

    def flip(c, bit):
        return c + bit * (1 - 2 * lax.rem(c // bit, 2))

    def chip_at(off):
        c = chip
        for j in range(steps):
            if off >> j & 1:
                c = flip(c, 1 << j)
        return c

    low = [1 << j for j in range(steps)]
    high = low[::-1]
    bits = [a + lane * (b - a) for a, b in zip(low, high)]
    partners = [flip(chip, a) + lane * (flip(chip, b) - flip(chip, a)) for a, b in zip(low, high)]

    def slot_of(code):
        return sum((bits[j] for j in range(steps) if code >> j & 1), 0)

    def remote(src, dst, ssem, rsem, seg_to, blk_to):
        return pltpu.make_async_remote_copy(
            src_ref=src,
            dst_ref=dst,
            send_sem=ssem,
            recv_sem=rsem,
            device_id=(seg_to, blk_to),
            device_id_type=MESH,
        )

    def cols(index):
        return pl.ds(pl.multiple_of(index * width, width), width)

    def span(index, size):
        return pl.ds(pl.multiple_of(index * size, size), size)

    def landed(ref, sem):
        remote(ref, ref, g0_send, sem, seg, mate).wait_recv()

    def loaded(ref, sem):
        pltpu.make_async_copy(ref, ref, sem).wait()

    racts = (racts0, racts1)
    a_recv = (a0_recv, a1_recv)

    def racts_at(slot, side, part_of):
        return racts[part_of].at[span(slot * 2 + side, tb if part_of == 0 else half)]

    def bulk(count):
        return core_all.at[pl.ds(0, count // 2), 0 : 2 * width]

    keep = pl.ds(pl.multiple_of(tb + lane * half, half), half)
    give = pl.ds(pl.multiple_of(tb + mate_lane * half, half), half)

    l_top = pltpu.make_async_copy(qtop_h, errs, load_sem.at[0])

    @pl.when(seg == segs - 1)
    def _():
        l_top.start()

    for src, dst, n in (
        (acts_h, acts, 2),
        (bin_h, b_in, 2),
        (back_h, back, 1),
        (deriv_h, deriv, 1),
        (counts_h, counts, 3),
        (grads_h.at[keep, :], own_g, 4),
        (bout_h, b_out, 5),
        (qacts_h, qacts, 5),
        (eig_h, eig, 6),
        (grads_h.at[pl.ds(0, tb), cols(blk)], grads0.at[span(lane, tb)], None),
    ):
        sem = early_recv.at[0] if n is None else load_sem.at[n]
        pltpu.make_async_copy(src, dst, sem).start()

    def e_copy(n):
        r = pl.ds(n * qt, qt)
        return remote(moved.at[r], errs.at[r], e_send, e_recv.at[n], below, blk)

    def advance(n):
        r = pl.ds(n * qt, qt)
        e = errs[r]
        mixed = jnp.dot(e, back[...], preferred_element_type=F32)
        moved[r] = (e.astype(F32) + mixed * deriv[r].astype(F32)).astype(B16)

    def relay(code, part_of):
        slot = slot_of(code)
        src = racts_at(slot, lane, part_of)
        for j in range(code.bit_length(), steps):
            to = slot + bits[j]
            dst, dest = racts_at(to, lane, part_of), partners[j] * 2 + lane
            remote(src, dst, a_send.at[part_of], a_recv[part_of].at[to], seg, dest).start()
        sem = late_recv if part_of else early_recv.at[slot]
        remote(src, src, a_send.at[part_of], sem, seg, mate).start()

    def handed_on(code, part_of):
        slot = slot_of(code)
        landed(racts_at(slot, lane, part_of), a_recv[part_of].at[slot])
        relay(code, part_of)

    def send0(off, chip_to, side):
        dest = chip_to * 2 + side
        remote(
            grads_h.at[pl.ds(0, tb), cols(dest)],
            grads0.at[span(off * 2 + lane, tb)],
            g0_send,
            early_recv.at[off],
            seg,
            dest,
        ).start()

    def send1(off, side):
        dest = chip_at(off) * 2 + side
        remote(
            own_g.at[:, cols(dest)],
            grads1.at[span(off * 2 + lane, half)],
            g1_send,
            late_recv,
            seg,
            dest,
        ).start()

    near = list(low)
    far = [off for off in range(1, chips) if off not in near]
    last_codes = list(range((1 << steps - 1) + 1, chips))
    first_codes = [code for code in range(1, chips) if code not in last_codes]

    loaded(bulk(width + rows), load_sem.at[2])
    racts0[span(lane, tb)] = jnp.dot(
        acts[0:tb], b_in[...], preferred_element_type=F32
    ).astype(B16)

    @pl.when(seg == segs - 1)
    def _():
        loaded(bulk(width + qrows), load_sem.at[1])
        l_top.wait()
        for n in range(queries // 2):
            advance(n)

    sides = (seg + segs - 1) // segs + (2 * segs - 2 - seg) // segs
    pl.semaphore_wait(barrier, blks - 1 + sides)

    remote(acts_h.at[give, :], other_a, g1_send, sel_recv.at[0], seg, mate).start()
    relay(0, 0)
    remote(grads_h.at[give, :], other_g, g1_send, sel_recv.at[1], seg, mate).start()

    @pl.when(seg == segs - 1)
    def _():
        for n in range(queries // 2):
            e_copy(n).start()
        for n in range(queries // 2, queries):
            advance(n)
            e_copy(n).start()

    loaded(counts, load_sem.at[3])
    full = counts[blk] == SLOTS
    landed(other_a, sel_recv.at[0])
    picked = jnp.where(full, acts[keep, :].astype(F32), other_a[...].astype(F32)).astype(B16)
    racts1[span(lane, half)] = jnp.dot(picked, b_in[...], preferred_element_type=F32).astype(B16)

    relay(0, 1)
    for j in range(steps - 1):
        send0(bits[j], partners[j], lane)
        send0(bits[j], partners[j], mate_lane)

    def tell_above():
        pl.semaphore_signal(ready, inc=1, device_id=(above, blk), device_id_type=MESH)

    pl.when(seg == 0)(tell_above)

    loaded(own_g, load_sem.at[4])
    landed(other_g, sel_recv.at[1])
    own_g[...] = jnp.where(full, own_g[...].astype(F32), other_g[...].astype(F32)).astype(B16)

    for code in first_codes:
        handed_on(code, 0)
    for code in first_codes:
        handed_on(code, 1)
    send0(bits[steps - 1], partners[steps - 1], lane)
    send0(bits[steps - 1], partners[steps - 1], mate_lane)
    for off in far:
        send0(off, chip_at(off), lane)
        send0(off, chip_at(off), mate_lane)
    send0(0, chip, mate_lane)
    for off in far + near:
        send1(off, lane)
        send1(off, mate_lane)
    send1(0, mate_lane)
    own1 = pltpu.make_async_copy(own_g.at[:, cols(blk)], grads1.at[span(lane, half)], late_recv)
    own1.start()

    @pl.when(jnp.logical_and(seg > 0, seg < segs - 1))
    def _():
        pl.semaphore_wait(ready, 1)
        tell_above()

    @pl.when(seg < segs - 1)
    def _():
        loaded(bulk(width + qrows), load_sem.at[1])

    @pl.when(jnp.logical_and(seg > 0, seg < segs - 1))
    def _():
        for n in range(queries):
            landed(errs.at[pl.ds(n * qt, qt)], e_recv.at[n])
            advance(n)
            e_copy(n).start()

    loaded(bulk(width + qrows), load_sem.at[5])
    rot_q[...] = jnp.dot(qacts[...], b_in[...], preferred_element_type=F32).astype(B16)
    loaded(eig, load_sem.at[6])
    inv = 1.0 / (eig[...].astype(F32) + damping)

    def relay_last():
        for code in last_codes:
            handed_on(code, 0)
            handed_on(code, 1)

    pl.when(seg == 0)(relay_last)

    for q in range(queries):

        @pl.when(seg == 0)
        def _():
            landed(errs.at[pl.ds(q * qt, qt)], e_recv.at[q])

        r = pl.ds(q * qt, qt)
        rot_e = jnp.dot(errs[r], b_out[...], preferred_element_type=F32).astype(B16)
        raw = lax.dot_general(
            rot_e, rot_q[r], (((0,), (0,)), ((), ())), preferred_element_type=F32
        )
        core_all[:, q * width : (q + 1) * width] = (raw * inv).astype(B16)

    pl.when(seg > 0)(relay_last)

    def core_of(q):
        return core_all[:, q * width : (q + 1) * width]

    def folded(x):
        x = sum(x[:, n * 128 : (n + 1) * 128] for n in range(width // 128))
        return jnp.sum(x, axis=0, keepdims=True)

    for pair in range(0, chips, 2):
        for i in (pair, pair + 1):
            landed(grads0.at[pl.ds(0, 3 * tb)], early_recv.at[i])
        here = pl.ds(pair * 2 * tb, 4 * tb)
        turned = jnp.dot(grads0[here, :], b_out[...], preferred_element_type=F32).astype(B16)
        for q in range(queries):
            h = jnp.dot(turned, core_of(q), preferred_element_type=F32)
            prod = h * racts0[here, :].astype(F32)
            for n in range(4):
                i, side = pair + n // 2, n % 2
                part[i, side, q : q + 1, :] = folded(prod[n * tb : (n + 1) * tb])

    landed(racts0.at[pl.ds(0, (blks + chips) * half)], late_recv)
    turned = jnp.dot(grads1[...], b_out[...], preferred_element_type=F32).astype(B16)
    for q in range(queries):
        h = jnp.dot(turned, core_of(q), preferred_element_type=F32)
        prod = h * racts1[...].astype(F32)
        for i in range(chips):
            shared = folded(prod[i * tb : (i + 1) * tb])
            for side in range(2):
                part[i, side, queries + q : queries + q + 1, :] = shared

    values = SLOTS * queries
    tile = (chips, 2, values, 128)
    diag = lax.broadcasted_iota(jnp.int32, tile, 2) == lax.broadcasted_iota(jnp.int32, tile, 3)
    sums = jnp.sum(part[...], axis=3, keepdims=True)
    packed[...] = jnp.sum(jnp.where(diag, sums, 0.0), axis=2, keepdims=True)

    @pl.when(seg == segs - 1)
    def _():
        pl.semaphore_wait(ready, 1)

    for seg_off in range(segs - 1, -1, -1):
        seg_to = lax.rem(seg + seg_off, segs)
        for off in range(chips - 1, -1, -1):
            chip_to = chip_at(off)
            for side in (lane, mate_lane):
                if seg_off == 0 and off == 0 and side is lane:
                    continue
                remote(
                    packed.at[off, side],
                    gathered.at[seg * blks + blk],
                    p_send,
                    p_recv,
                    seg_to,
                    chip_to * 2 + side,
                ).start()
    gathered[seg * blks + blk] = packed[0, lane]
    others = gathered.at[pl.ds(0, segs * blks - 1)]
    landed(others, p_recv)
    total = jnp.sum(gathered[...].reshape(segs * blks, 128), axis=0, keepdims=True)
    tile = (values, 128)
    row = lax.broadcasted_iota(jnp.int32, tile, 0)
    col = lax.broadcasted_iota(jnp.int32, tile, 1)
    spread = jnp.where(row == col, jnp.broadcast_to(total, tile), 0.0)
    spread = jnp.sum(spread, axis=1, keepdims=True)
    spread = jnp.where(lax.rem(row, queries) == col, jnp.broadcast_to(spread, tile), 0.0)
    for n in range(SLOTS):
        scores = jnp.sum(
            jnp.where(row // queries == n, spread, 0.0), axis=0, keepdims=True
        )[:, 0:queries]
        out[n : n + 1, :] = scores * jnp.where(full, 1.0, 0.0) if n else scores

    remote(others, others, p_send, p_recv, seg, mate).wait_send()

    def sent(count, sem):
        ref = racts0.at[pl.ds(0, count)]
        remote(ref, ref, sem, sel_recv.at[0], seg, mate).wait_send()

    sent((blks - 1) * tb, g0_send)
    sent((blks - 1) * half + half + half * blks, g1_send)
    sent((2 * chips - 1) * tb, a_send.at[0])
    sent((2 * chips - 1) * half, a_send.at[1])

    @pl.when(seg > 0)
    def _():
        sent(qrows, e_send)


def body(
    train_acts,
    train_grads,
    counts,
    basis_in,
    basis_out,
    eigenvalues,
    back_weight,
    derivative,
    query_acts,
    query_top,
):
    segs = lax.axis_size("seg")
    blks = lax.axis_size("blk")
    chips = blks // 2
    queries, qt, width = query_top.shape
    rows = train_acts.shape[1]
    tb = rows // SLOTS
    half = tb // 2
    wide = train_grads.shape[2]
    any_spec = pl.BlockSpec(memory_space=pltpu.HBM)
    vm = pltpu.VMEM
    dma = pltpu.SemaphoreType.DMA
    result = pl.pallas_call(
        functools.partial(kernel, segs, blks, queries),
        out_shape=pltpu.VMEM((SLOTS, queries), F32),
        in_specs=[any_spec] * 10,
        out_specs=pl.BlockSpec(memory_space=pltpu.VMEM),
        scratch_shapes=[
            pltpu.SMEM(counts.shape, counts.dtype),
            vm((rows, width), B16),
            vm((half, wide), B16),
            vm((half, wide), B16),
            vm((half, width), B16),
            vm((width, width), B16),
            vm((width, width), B16),
            vm((width, width), B16),
            vm((width, width), B16),
            vm((queries * qt, width), B16),
            vm((queries * qt, width), B16),
            vm((queries * qt, width), B16),
            vm((queries * qt, width), B16),
            vm((queries * qt, width), B16),
            vm((width, queries * width), B16),
            vm((blks * tb, width), B16),
            vm((blks * half, width), B16),
            vm((blks * tb, width), B16),
            vm((blks * half, width), B16),
            vm((chips, 2, SLOTS * queries, 128), F32),
            vm((chips, 2, 1, 128), F32),
            vm((segs * blks, 1, 128), F32),
            dma((7,)),
            dma((2,)),
            dma(()),
            dma(()),
            dma((2,)),
            dma((chips,)),
            dma(()),
            dma((chips,)),
            dma((chips,)),
            dma(()),
            dma((queries,)),
            dma(()),
            dma(()),
            pltpu.SemaphoreType.REGULAR,
        ],
        compiler_params=pltpu.CompilerParams(
            collective_id=0, has_side_effects=True, vmem_limit_bytes=67_043_328 - 32_768
        ),
    )(
        counts,
        train_acts[0],
        train_grads[0],
        basis_in[0, 0],
        basis_out[0, 0],
        eigenvalues[0, 0],
        back_weight[0, 0],
        derivative[0].reshape(queries * qt, width),
        query_acts[0].reshape(queries * qt, width),
        query_top.reshape(queries * qt, width),
    )
    return result.T


def solution(mesh):
    in_specs = (
        P("seg", "blk", None),
        P("seg", "blk", None),
        P(),
        P("seg", None, None, None),
        P("seg", "blk", None, None),
        P("seg", "blk", None, None),
        P("seg", "blk", None, None),
        P("seg", None, None, "blk"),
        P("seg", None, None, None),
        P(None, None, "blk"),
    )
    out_specs = P(None, "blk")
    return jax.shard_map(body, mesh=mesh, in_specs=in_specs, out_specs=out_specs, check_vma=False)
```

time: 27.2 us -> 25.9 us (0.952)
  Pallas kernels: 26.5 us -> 25.2 us
    pallas_call x1, Pallas kernels: 26.5 us -> 25.2 us  [body(): pl.pallas_call(functools.partial(kernel, segs, blks, queries), out_shape=...]
where the time goes in v2:
time: 25.9 us; the launch traced here: 25.7 us
  Pallas kernels  25.2 us (97%)
  local copies, waits for them, and re-layouts  0.56 us (2%)
    pallas_call x1, Pallas kernels, body(): pl.pallas_call(functools.partial(kernel, segs, blks, queries), out_shape=...  25.2 us
    unnamed x1, local copies, waits for them, and re-layouts  0.56 us

profile of v2, /device:TPU:0, one launch (start us, length us, event | category | flops | bytes accessed | tf_op | source)
XLA Modules:
  0.0 25.7 jit_solution(12773114851564168918)
XLA Ops:
  0.0 25.2 %shard_map.100 = f32[2,4]{1,0:T(2,128)S(1)} custom-call(s32[8]{0:T(128)} %counts_h.1, bf16[128,512]{1,0:T(8,128)(2,1)} %bitcast.16, bf16[128,4096]{1,0:T(8,128)(2,1)} %bitcast.11, bf16[512,512]{1,0:T(8,128)(2,1)} %bitcast.12, bf16[512,512]{1,0:T(8,128)(2,1)} %bitcast.13, bf16[512,512]{1,0:T(8,128)(2,1)} %bitcast.14, bf16[512,512]{1,0:T(8,128)(2,1)} %bitcast.15, ...), custom_call_target="tpu_custom_call" | custom-call | tf_op jit(solution)/shard_map/pallas_call | solution.py:440
  25.2 0.6 %copy.12 = f32[4,2]{0,1:T(2,128)} copy(f32[4,2]{0,1:T(2,128)S(1)} %bitcast.10) | data formatting | bytes 64

commit v3 on v2

--- a/solution.py
+++ b/solution.py
@@ -148,26 +148,19 @@
     keep = pl.ds(pl.multiple_of(tb + lane * half, half), half)
     give = pl.ds(pl.multiple_of(tb + mate_lane * half, half), half)
 
-    l_top = pltpu.make_async_copy(qtop_h, errs, load_sem.at[0])
+    def load(src, dst, sem):
+        pltpu.make_async_copy(src, dst, sem).start()
+
+    load(acts_h, acts, load_sem.at[2])
+    load(bin_h, b_in, load_sem.at[2])
+    load(counts_h, counts, load_sem.at[3])
+    load(grads_h.at[keep, :], own_g, load_sem.at[4])
 
     @pl.when(seg == segs - 1)
     def _():
-        l_top.start()
-
-    for src, dst, n in (
-        (acts_h, acts, 2),
-        (bin_h, b_in, 2),
-        (back_h, back, 1),
-        (deriv_h, deriv, 1),
-        (counts_h, counts, 3),
-        (grads_h.at[keep, :], own_g, 4),
-        (bout_h, b_out, 5),
-        (qacts_h, qacts, 5),
-        (eig_h, eig, 6),
-        (grads_h.at[pl.ds(0, tb), cols(blk)], grads0.at[span(lane, tb)], None),
-    ):
-        sem = early_recv.at[0] if n is None else load_sem.at[n]
-        pltpu.make_async_copy(src, dst, sem).start()
+        load(back_h, back, load_sem.at[1])
+        load(deriv_h, deriv, load_sem.at[1])
+        load(qtop_h, errs, load_sem.at[0])
 
     def e_copy(n):
         r = pl.ds(n * qt, qt)
@@ -226,13 +219,6 @@
         acts[0:tb], b_in[...], preferred_element_type=F32
     ).astype(B16)
 
-    @pl.when(seg == segs - 1)
-    def _():
-        loaded(bulk(width + qrows), load_sem.at[1])
-        l_top.wait()
-        for n in range(queries // 2):
-            advance(n)
-
     sides = (seg + segs - 1) // segs + (2 * segs - 2 - seg) // segs
     pl.semaphore_wait(barrier, blks - 1 + sides)
 
@@ -242,11 +228,21 @@
 
     @pl.when(seg == segs - 1)
     def _():
-        for n in range(queries // 2):
-            e_copy(n).start()
-        for n in range(queries // 2, queries):
+        loaded(bulk(width + qrows), load_sem.at[1])
+        loaded(errs, load_sem.at[0])
+        for n in range(queries):
             advance(n)
             e_copy(n).start()
+
+    @pl.when(seg < segs - 1)
+    def _():
+        load(back_h, back, load_sem.at[1])
+        load(deriv_h, deriv, load_sem.at[1])
+
+    load(bout_h, b_out, load_sem.at[5])
+    load(qacts_h, qacts, load_sem.at[5])
+    load(eig_h, eig, load_sem.at[6])
+    load(grads_h.at[pl.ds(0, tb), cols(blk)], grads0.at[span(lane, tb)], early_recv.at[0])
 
     loaded(counts, load_sem.at[3])
     full = counts[blk] == SLOTS
@@ -268,15 +264,21 @@
     landed(other_g, sel_recv.at[1])
     own_g[...] = jnp.where(full, own_g[...].astype(F32), other_g[...].astype(F32)).astype(B16)
 
+    def chain():
+        loaded(bulk(width + qrows), load_sem.at[1])
+        for n in range(queries):
+            landed(errs.at[pl.ds(n * qt, qt)], e_recv.at[n])
+            advance(n)
+            e_copy(n).start()
+
     for code in first_codes:
         handed_on(code, 0)
     for code in first_codes:
         handed_on(code, 1)
-    send0(bits[steps - 1], partners[steps - 1], lane)
-    send0(bits[steps - 1], partners[steps - 1], mate_lane)
-    for off in far:
-        send0(off, chip_at(off), lane)
-        send0(off, chip_at(off), mate_lane)
+    for side in (lane, mate_lane):
+        for off in far:
+            send0(off, chip_at(off), side)
+        send0(bits[steps - 1], partners[steps - 1], side)
     send0(0, chip, mate_lane)
     for off in far + near:
         send1(off, lane)
@@ -290,16 +292,11 @@
         pl.semaphore_wait(ready, 1)
         tell_above()
 
-    @pl.when(seg < segs - 1)
+    pl.when(jnp.logical_and(seg > 0, seg < segs - 1))(chain)
+
+    @pl.when(seg == 0)
     def _():
         loaded(bulk(width + qrows), load_sem.at[1])
-
-    @pl.when(jnp.logical_and(seg > 0, seg < segs - 1))
-    def _():
-        for n in range(queries):
-            landed(errs.at[pl.ds(n * qt, qt)], e_recv.at[n])
-            advance(n)
-            e_copy(n).start()
 
     loaded(bulk(width + qrows), load_sem.at[5])
     rot_q[...] = jnp.dot(qacts[...], b_in[...], preferred_element_type=F32).astype(B16)

time: 25.9 us -> 25.8 us (level)
  no operation moved by 1% of the time
where the time goes in v3:
time: 25.8 us; the launch traced here: 25.7 us
  Pallas kernels  25.1 us (97%)
  local copies, waits for them, and re-layouts  0.56 us (2%)
    pallas_call x1, Pallas kernels, body(): pl.pallas_call(functools.partial(kernel, segs, blks, queries), out_shape=...  25.1 us
    unnamed x1, local copies, waits for them, and re-layouts  0.56 us

profile of v3, /device:TPU:0, one launch (start us, length us, event | category | flops | bytes accessed | tf_op | source)
XLA Modules:
  0.0 25.7 jit_solution(7360353662004824890)
XLA Ops:
  0.0 25.1 %shard_map.100 = f32[2,4]{1,0:T(2,128)S(1)} custom-call(s32[8]{0:T(128)} %counts_h.1, bf16[128,512]{1,0:T(8,128)(2,1)} %bitcast.16, bf16[128,4096]{1,0:T(8,128)(2,1)} %bitcast.11, bf16[512,512]{1,0:T(8,128)(2,1)} %bitcast.12, bf16[512,512]{1,0:T(8,128)(2,1)} %bitcast.13, bf16[512,512]{1,0:T(8,128)(2,1)} %bitcast.14, bf16[512,512]{1,0:T(8,128)(2,1)} %bitcast.15, ...), custom_call_target="tpu_custom_call" | custom-call | tf_op jit(solution)/shard_map/pallas_call | solution.py:437
  25.1 0.6 %copy.12 = f32[4,2]{0,1:T(2,128)} copy(f32[4,2]{0,1:T(2,128)S(1)} %bitcast.10) | data formatting | bytes 64
